TPU v7x, 512 devices: a whole 4x8x8 slice. The times are simulated.
512 devices in a mesh: section: 4 (over x), space: 128 (over y, z, core).
Axes of the slice: x: 4, y: 8, z: 8, core: 2. Of those that a mesh axis runs over, the one named last changes fastest.
Arguments:
- raster: bfloat16 [4, 512, 128, 256], P(None, 'space'), may hold values from -6 to 6
- row_coef: bfloat16 [4, 15, 512, 128], P('section', None, 'space'), may hold values from -1.5 to 1.5
- col_coef: bfloat16 [4, 15, 128, 512], P('section', None, 'space'), may hold values from -1.5 to 1.5
- norm_gain: bfloat16 [4, 256], P('section'), may hold values from 0.099609375 to 1.8984375
- weight_in: bfloat16 [4, 256, 512], P('section'), may hold values from -0.375 to 0.375
- bias_in: bfloat16 [4, 512], P('section'), may hold values from -3 to 3
- weight_out: bfloat16 [4, 512, 256], P('section'), may hold values from -0.25 to 0.25
- readout: bfloat16 [256], replicated, may hold values from -0.375 to 0.375
Outputs:
- density: float32 [4, 512, 128], P('section', 'space')
All inputs are finite; a program needn't handle non-finite values.
Results may differ from a plain program's by a relative error of at most 0.015.
Values may be sent and summed in bfloat16 or wider, within the bound.
A program may use at most 64 MiB of HBM per device.

v0:
```python
import jax
import jax.numpy as jnp
from jax import lax
from jax.sharding import PartitionSpec as P


def from_behind(array, axis, by):
    size = lax.axis_size(axis)
    pairs = [(i, i + by) for i in range(size) if 0 <= i + by < size]
    return lax.ppermute(array, axis, pairs)


def from_root(value, axis, source):
    kept = jnp.where(lax.axis_index(axis) == source, value, 0).astype(value.dtype)
    return lax.psum(kept, axis)


def row_stencil(surface, coefficients):
    taps_count = coefficients.shape[0]
    radius = taps_count // 2
    columns = surface.shape[1]
    padded = jnp.pad(surface.astype(jnp.float32), ((0, 0), (radius, radius), (0, 0)))
    summed = jnp.zeros(surface.shape, jnp.float32)
    for offset in range(taps_count):
        summed = (
            summed
            + coefficients[offset].astype(jnp.float32)[:, :, None]
            * padded[:, offset : offset + columns, :]
        )
    return summed


def col_stencil(surface, coefficients):
    taps_count = coefficients.shape[0]
    radius = taps_count // 2
    lines = surface.shape[0]
    swapped = jnp.swapaxes(coefficients, 1, 2)
    padded = jnp.pad(surface.astype(jnp.float32), ((radius, radius), (0, 0), (0, 0)))
    summed = jnp.zeros(surface.shape, jnp.float32)
    for offset in range(taps_count):
        summed = (
            summed
            + swapped[offset].astype(jnp.float32)[:, :, None]
            * padded[offset : offset + lines, :, :]
        )
    return summed


def apply_layer(current, params):
    row_part = row_stencil(current, params[0]).astype(jnp.bfloat16)
    columns_view = lax.all_to_all(row_part, "space", split_axis=1, concat_axis=0, tiled=True)
    mixed_field = col_stencil(columns_view, params[1])
    inverse = lax.rsqrt(jnp.mean(mixed_field * mixed_field, axis=-1, keepdims=True) + 1e-06)
    normed = (mixed_field * inverse * params[2].astype(jnp.float32)).astype(jnp.bfloat16)
    hidden = jax.nn.gelu(
        jnp.dot(normed, params[3], preferred_element_type=jnp.float32)
        + params[4].astype(jnp.float32),
        approximate=True,
    ).astype(jnp.bfloat16)
    return (mixed_field + jnp.dot(hidden, params[5], preferred_element_type=jnp.float32)).astype(
        jnp.bfloat16
    )


def to_rows(output):
    return lax.all_to_all(output, "space", split_axis=0, concat_axis=1, tiled=True)


def read_density(output, readout):
    return jax.nn.softplus(jnp.dot(output, readout, preferred_element_type=jnp.float32))


def on_device(raster, row_coef, col_coef, norm_gain, weight_in, bias_in, weight_out, readout):
    sections = lax.axis_size("section")
    spaces = lax.axis_size("space")
    windows = raster.shape[0]
    position = lax.axis_index("section")
    params = (row_coef[0], col_coef[0], norm_gain[0], weight_in[0], bias_in[0], weight_out[0])
    carried = jnp.zeros(raster.shape[1:], jnp.bfloat16)
    finished = jnp.zeros(
        (windows, raster.shape[1] * spaces, raster.shape[2] // spaces), jnp.float32
    )
    for moment in range(windows + sections - 1):
        entering = raster[min(moment, windows - 1)]
        current = jnp.where(position == 0, entering, carried)
        output = apply_layer(current, params)
        finished_index = moment - (sections - 1)
        if finished_index >= 0:
            finished = finished.at[finished_index].set(read_density(output, readout))
        if moment < windows + sections - 2:
            carried = from_behind(to_rows(output), "section", 1)
    row_density = lax.all_to_all(finished, "space", split_axis=1, concat_axis=2, tiled=True)
    everyone = from_root(row_density, "section", sections - 1)
    return lax.dynamic_slice_in_dim(everyone, position, 1, 0)


def solution(mesh):
    placed = (
        P(None, "space", None, None),
        P("section", None, "space", None),
        P("section", None, "space", None),
        P("section", None),
        P("section", None, None),
        P("section", None),
        P("section", None, None),
        P(),
    )
    return jax.shard_map(
        on_device,
        mesh=mesh,
        in_specs=placed,
        out_specs=P("section", "space", None),
        check_vma=False,
    )
```

profile of v0, /device:TPU:8, one launch (start us, length us, event | category | flops | bytes accessed | tf_op | source)
XLA Modules:
  0.0 451.9 jit_solution(15485702138309507935)
XLA Ops:
  0.0 1.3 fusion.370
  3.2 4.4 add_convert_fusion.6
  7.7 17.5 %all-to-all-start = ((bf16[4,128,256]{2,0,1:T(4,128)(2,1)}), bf16[4,128,256]{2,0,1:T(4,128)(2,1)S(1)}, u32[]{:S(2)}, u32[]{:S(2)}) async-start(bf16[4,128,256]{2,0,1:T(4,128)(2,1)} %add_convert_fusion.6), calls=%async_computation | async-start | bytes 524288 | tf_op jit(solution)/shard_map/all_to_all | solution.py:51
  25.9 14.0 %all-to-all-done = bf16[4,128,256]{2,0,1:T(4,128)(2,1)S(1)} async-done(((bf16[4,128,256]{2,0,1:T(4,128)(2,1)}), bf16[4,128,256]{2,0,1:T(4,128)(2,1)S(1)}, u32[]{:S(2)}, u32[]{:S(2)}) %all-to-all-start) | async-done | bytes 262176 | tf_op jit(solution)/shard_map/all_to_all | solution.py:51
  40.2 1.7 multiply_reduce_fusion.6
  41.9 0.7 fusion.13
  43.1 0.8 reduce.21
  44.1 20.6 %all_to_all.180 = bf16[128,2,512]{2,1,0:T(2,128)(2,1)S(1)} all-to-all(bf16[128,2,512]{2,1,0:T(2,128)(2,1)S(1)} %reshape.1147), channel_id=1, replica_groups=mesh['section'=4,'space'=128] {'space'}, dimensions={0} | all-to-all | bytes 524288 | tf_op jit(solution)/shard_map/all_to_all | solution.py:66
  64.9 1.6 reduce.15
  66.6 3.4 collective-permute-start
  70.0 4.9 %collective-permute-done = bf16[4,128,256]{2,0,1:T(4,128)(2,1)S(1)} collective-permute-done((bf16[4,128,256]{2,0,1:T(4,128)(2,1)S(1)}, bf16[4,128,256]{2,0,1:T(4,128)(2,1)S(1)}, u32[]{:S(2)}, u32[]{:S(2)}) %collective-permute-start) | collective-permute-done | bytes 262176 | tf_op jit(solution)/shard_map/ppermute | solution.py:10
  75.1 3.3 add_convert_fusion.5
  78.4 21.4 %all_to_all.181 = bf16[4,128,256]{2,0,1:T(4,128)(2,1)S(1)} all-to-all(bf16[4,128,256]{2,0,1:T(4,128)(2,1)S(1)} %add_convert_fusion.5), channel_id=1, replica_groups=mesh['section'=4,'space'=128] {'space'}, dimensions={1} | all-to-all | bytes 524288 | tf_op jit(solution)/shard_map/all_to_all | solution.py:51
  100.1 1.7 multiply_reduce_fusion.5
  102.5 0.8 reduce.22
  103.5 20.6 %all_to_all.182 = bf16[128,2,512]{2,1,0:T(2,128)(2,1)S(1)} all-to-all(bf16[128,2,512]{2,1,0:T(2,128)(2,1)S(1)} %reshape.1149), channel_id=1, replica_groups=mesh['section'=4,'space'=128] {'space'}, dimensions={0} | all-to-all | bytes 524288 | tf_op jit(solution)/shard_map/all_to_all | solution.py:66
  124.3 1.6 reduce.16
  126.0 4.4 collective-permute-start.1
  130.4 4.9 %collective-permute-done.1 = bf16[4,128,256]{2,0,1:T(4,128)(2,1)S(1)} collective-permute-done((bf16[4,128,256]{2,0,1:T(4,128)(2,1)S(1)}, bf16[4,128,256]{2,0,1:T(4,128)(2,1)S(1)}, u32[]{:S(2)}, u32[]{:S(2)}) %collective-permute-start.1) | collective-permute-done | bytes 262176 | tf_op jit(solution)/shard_map/ppermute | solution.py:10
  135.5 3.3 add_convert_fusion.4
  138.8 20.9 %all_to_all.183 = bf16[4,128,256]{2,0,1:T(4,128)(2,1)S(1)} all-to-all(bf16[4,128,256]{2,0,1:T(4,128)(2,1)S(1)} %add_convert_fusion.4), channel_id=1, replica_groups=mesh['section'=4,'space'=128] {'space'}, dimensions={1} | all-to-all | bytes 524288 | tf_op jit(solution)/shard_map/all_to_all | solution.py:51
  160.0 1.7 multiply_reduce_fusion.4
  162.4 0.8 reduce.23
  163.4 20.8 %all_to_all.184 = bf16[128,2,512]{2,1,0:T(2,128)(2,1)S(1)} all-to-all(bf16[128,2,512]{2,1,0:T(2,128)(2,1)S(1)} %reshape.1151), channel_id=1, replica_groups=mesh['section'=4,'space'=128] {'space'}, dimensions={0} | all-to-all | bytes 524288 | tf_op jit(solution)/shard_map/all_to_all | solution.py:66
  184.4 1.6 reduce.17
  186.0 4.4 collective-permute-start.2
  190.4 4.7 %collective-permute-done.2 = bf16[4,128,256]{2,0,1:T(4,128)(2,1)S(1)} collective-permute-done((bf16[4,128,256]{2,0,1:T(4,128)(2,1)S(1)}, bf16[4,128,256]{2,0,1:T(4,128)(2,1)S(1)}, u32[]{:S(2)}, u32[]{:S(2)}) %collective-permute-start.2) | collective-permute-done | bytes 262176 | tf_op jit(solution)/shard_map/ppermute | solution.py:10
  195.4 3.3 add_convert_fusion.3
  198.7 21.1 %all_to_all.185 = bf16[4,128,256]{2,0,1:T(4,128)(2,1)S(1)} all-to-all(bf16[4,128,256]{2,0,1:T(4,128)(2,1)S(1)} %add_convert_fusion.3), channel_id=1, replica_groups=mesh['section'=4,'space'=128] {'space'}, dimensions={1} | all-to-all | bytes 524288 | tf_op jit(solution)/shard_map/all_to_all | solution.py:51
  220.1 1.7 multiply_reduce_fusion.3
  222.4 0.8 reduce.24
  223.4 20.6 %all_to_all.186 = bf16[128,2,512]{2,1,0:T(2,128)(2,1)S(1)} all-to-all(bf16[128,2,512]{2,1,0:T(2,128)(2,1)S(1)} %reshape.1153), channel_id=1, replica_groups=mesh['section'=4,'space'=128] {'space'}, dimensions={0} | all-to-all | bytes 524288 | tf_op jit(solution)/shard_map/all_to_all | solution.py:66
  244.3 1.6 reduce.18
  245.9 4.4 collective-permute-start.3
  250.3 4.9 %collective-permute-done.3 = bf16[4,128,256]{2,0,1:T(4,128)(2,1)S(1)} collective-permute-done((bf16[4,128,256]{2,0,1:T(4,128)(2,1)S(1)}, bf16[4,128,256]{2,0,1:T(4,128)(2,1)S(1)}, u32[]{:S(2)}, u32[]{:S(2)}) %collective-permute-start.3) | collective-permute-done | bytes 262176 | tf_op jit(solution)/shard_map/ppermute | solution.py:10
  255.4 3.3 add_convert_fusion.2
  258.8 20.9 %all_to_all.187 = bf16[4,128,256]{2,0,1:T(4,128)(2,1)S(1)} all-to-all(bf16[4,128,256]{2,0,1:T(4,128)(2,1)S(1)} %add_convert_fusion.2), channel_id=1, replica_groups=mesh['section'=4,'space'=128] {'space'}, dimensions={1} | all-to-all | bytes 524288 | tf_op jit(solution)/shard_map/all_to_all | solution.py:51
  280.0 1.7 multiply_reduce_fusion.2
  282.3 0.8 reduce.25
  283.3 20.6 %all_to_all.188 = bf16[128,2,512]{2,1,0:T(2,128)(2,1)S(1)} all-to-all(bf16[128,2,512]{2,1,0:T(2,128)(2,1)S(1)} %reshape.1155), channel_id=1, replica_groups=mesh['section'=4,'space'=128] {'space'}, dimensions={0} | all-to-all | bytes 524288 | tf_op jit(solution)/shard_map/all_to_all | solution.py:66
  304.2 1.6 reduce.19
  305.8 4.4 collective-permute-start.4
  310.2 4.9 %collective-permute-done.4 = bf16[4,128,256]{2,0,1:T(4,128)(2,1)S(1)} collective-permute-done((bf16[4,128,256]{2,0,1:T(4,128)(2,1)S(1)}, bf16[4,128,256]{2,0,1:T(4,128)(2,1)S(1)}, u32[]{:S(2)}, u32[]{:S(2)}) %collective-permute-start.4) | collective-permute-done | bytes 262176 | tf_op jit(solution)/shard_map/ppermute | solution.py:10
  315.3 4.4 add_convert_fusion.1
  319.8 6.5 %all-to-all-start.10 = ((bf16[4,128,256]{2,0,1:T(4,128)(2,1)}), bf16[4,128,256]{2,0,1:T(4,128)(2,1)S(1)}, u32[]{:S(2)}, u32[]{:S(2)}) async-start(bf16[4,128,256]{2,0,1:T(4,128)(2,1)} %add_convert_fusion.1), calls=%async_computation.10 | async-start | bytes 524288 | tf_op jit(solution)/shard_map/all_to_all | solution.py:51
  326.3 14.7 %all-to-all-done.10 = bf16[4,128,256]{2,0,1:T(4,128)(2,1)S(1)} async-done(((bf16[4,128,256]{2,0,1:T(4,128)(2,1)}), bf16[4,128,256]{2,0,1:T(4,128)(2,1)S(1)}, u32[]{:S(2)}, u32[]{:S(2)}) %all-to-all-start.10) | async-done | bytes 262176 | tf_op jit(solution)/shard_map/all_to_all | solution.py:51
  341.3 1.7 multiply_reduce_fusion.1
  343.7 0.8 reduce.26
  344.5 0.9 reshape.1157
  345.3 6.8 %all-to-all-start.11 = ((bf16[128,2,512]{2,1,0:T(2,128)(2,1)}), bf16[128,2,512]{2,1,0:T(2,128)(2,1)S(1)}, u32[]{:S(2)}, u32[]{:S(2)}) async-start(bf16[128,2,512]{2,1,0:T(2,128)(2,1)} %reshape.1157), calls=%async_computation.11 | async-start | bytes 524288 | tf_op jit(solution)/shard_map/all_to_all | solution.py:66
  352.5 14.4 %all-to-all-done.11 = bf16[128,2,512]{2,1,0:T(2,128)(2,1)S(1)} async-done(((bf16[128,2,512]{2,1,0:T(2,128)(2,1)}), bf16[128,2,512]{2,1,0:T(2,128)(2,1)S(1)}, u32[]{:S(2)}, u32[]{:S(2)}) %all-to-all-start.11) | async-done | bytes 262176 | tf_op jit(solution)/shard_map/all_to_all | solution.py:66
  367.1 1.6 reduce.20
  368.7 4.4 collective-permute-start.5
  373.2 4.9 %collective-permute-done.5 = bf16[4,128,256]{2,0,1:T(4,128)(2,1)S(1)} collective-permute-done((bf16[4,128,256]{2,0,1:T(4,128)(2,1)S(1)}, bf16[4,128,256]{2,0,1:T(4,128)(2,1)S(1)}, u32[]{:S(2)}, u32[]{:S(2)}) %collective-permute-start.5) | collective-permute-done | bytes 262176 | tf_op jit(solution)/shard_map/ppermute | solution.py:10
  378.3 4.4 add_convert_fusion
  382.7 6.4 %all-to-all-start.12 = ((bf16[4,128,256]{2,0,1:T(4,128)(2,1)}), bf16[4,128,256]{2,0,1:T(4,128)(2,1)S(1)}, u32[]{:S(2)}, u32[]{:S(2)}) async-start(bf16[4,128,256]{2,0,1:T(4,128)(2,1)} %add_convert_fusion), calls=%async_computation.12 | async-start | bytes 524288 | tf_op jit(solution)/shard_map/all_to_all | solution.py:51
  389.3 14.5 %all-to-all-done.12 = bf16[4,128,256]{2,0,1:T(4,128)(2,1)S(1)} async-done(((bf16[4,128,256]{2,0,1:T(4,128)(2,1)}), bf16[4,128,256]{2,0,1:T(4,128)(2,1)S(1)}, u32[]{:S(2)}, u32[]{:S(2)}) %all-to-all-start.12) | async-done | bytes 262176 | tf_op jit(solution)/shard_map/all_to_all | solution.py:51
  404.1 1.7 multiply_reduce_fusion
  405.8 0.7 fusion.14
  406.7 0.9 copy.117
  407.5 6.5 %all-to-all-start.13 = ((f32[4,512,1]{0,2,1:T(1,128)}), f32[4,512,1]{0,2,1:T(1,128)S(1)}, u32[]{:S(2)}, u32[]{:S(2)}) async-start(f32[4,512,1]{0,2,1:T(1,128)} %copy.117), calls=%async_computation.13 | async-start | bytes 524288 | tf_op jit(solution)/shard_map/all_to_all | solution.py:92
  414.1 14.7 %all-to-all-done.13 = f32[4,512,1]{0,2,1:T(1,128)S(1)} async-done(((f32[4,512,1]{0,2,1:T(1,128)}), f32[4,512,1]{0,2,1:T(1,128)S(1)}, u32[]{:S(2)}, u32[]{:S(2)}) %all-to-all-start.13) | async-done | bytes 8224 | tf_op jit(solution)/shard_map/all_to_all | solution.py:92
  429.0 1.0 copy.120
  430.1 20.7 %psum.7 = f32[4,4,128]{1,2,0:T(8,128)S(1)} all-reduce(f32[4,4,128]{1,2,0:T(8,128)S(1)} %bitcast.294), channel_id=1, replica_groups=mesh['section'=4,'space'=128] {'section'}, use_global_device_ids=true, to_apply=%region_7.8 | all-reduce | flops 2048 | bytes 16384 | tf_op jit(solution)/shard_map/psum | solution.py:15
  (100 shorter events, 13.8 us)
Async XLA Ops:
  0.0 41.9 %copy-start = (bf16[1,512,256]{2,1,0:T(8,128)(2,1)S(1)}, bf16[1,512,256]{2,1,0:T(8,128)(2,1)}, u32[]{:S(2)}) copy-start(bf16[1,512,256]{2,1,0:T(8,128)(2,1)} %param.22) | copy-start | bytes 786436
  0.0 1.3 copy-start.2
  7.7 17.5 %copy-start.3 = (bf16[1,512]{1,0:T(2,128)(2,1)S(1)}, bf16[1,512]{1,0:T(2,128)(2,1)}, u32[]{:S(2)}) copy-start(bf16[1,512]{1,0:T(2,128)(2,1)} %param.21) | copy-start | bytes 3076
  7.7 18.2 %copy-start.1 = (bf16[1,15,1,512]{3,1,2,0:T(8,128)(2,1)S(1)}, bf16[1,15,1,512]{3,1,2,0:T(8,128)(2,1)}, u32[]{:S(2)}) copy-start(bf16[1,15,1,512]{3,1,2,0:T(8,128)(2,1)} %param.18) | copy-start | bytes 46084
  7.7 32.2 %all-to-all-start = ((bf16[4,128,256]{2,0,1:T(4,128)(2,1)}), bf16[4,128,256]{2,0,1:T(4,128)(2,1)S(1)}, u32[]{:S(2)}, u32[]{:S(2)}) async-start(bf16[4,128,256]{2,0,1:T(4,128)(2,1)} %add_convert_fusion.6), calls=%async_computation | async-start | bytes 524288 | tf_op jit(solution)/shard_map/all_to_all | solution.py:51
  25.2 0.7 copy-start.4
  40.2 1.7 copy-start.5
  66.6 8.3 %collective-permute-start = (bf16[4,128,256]{2,0,1:T(4,128)(2,1)S(1)}, bf16[4,128,256]{2,0,1:T(4,128)(2,1)S(1)}, u32[]{:S(2)}, u32[]{:S(2)}) collective-permute-start(bf16[4,128,256]{2,0,1:T(4,128)(2,1)S(1)} %bitcast.296), channel_id=1, source_target_pairs={{0,128},{128,256},{256,384},{1,129},{129,257},{257,385},{2,130},{1... | collective-permute-start | bytes 786440 | tf_op jit(solution)/shard_map/ppermute | solution.py:10
  126.0 9.3 %collective-permute-start.1 = (bf16[4,128,256]{2,0,1:T(4,128)(2,1)S(1)}, bf16[4,128,256]{2,0,1:T(4,128)(2,1)S(1)}, u32[]{:S(2)}, u32[]{:S(2)}) collective-permute-start(bf16[4,128,256]{2,0,1:T(4,128)(2,1)S(1)} %bitcast.297), channel_id=1, source_target_pairs={{0,128},{128,256},{256,384},{1,129},{129,257},{257,385},{2,130},{1... | collective-permute-start | bytes 786440 | tf_op jit(solution)/shard_map/ppermute | solution.py:10
  186.0 9.1 %collective-permute-start.2 = (bf16[4,128,256]{2,0,1:T(4,128)(2,1)S(1)}, bf16[4,128,256]{2,0,1:T(4,128)(2,1)S(1)}, u32[]{:S(2)}, u32[]{:S(2)}) collective-permute-start(bf16[4,128,256]{2,0,1:T(4,128)(2,1)S(1)} %bitcast.298), channel_id=1, source_target_pairs={{0,128},{128,256},{256,384},{1,129},{129,257},{257,385},{2,130},{1... | collective-permute-start | bytes 786440 | tf_op jit(solution)/shard_map/ppermute | solution.py:10
  245.9 9.3 %collective-permute-start.3 = (bf16[4,128,256]{2,0,1:T(4,128)(2,1)S(1)}, bf16[4,128,256]{2,0,1:T(4,128)(2,1)S(1)}, u32[]{:S(2)}, u32[]{:S(2)}) collective-permute-start(bf16[4,128,256]{2,0,1:T(4,128)(2,1)S(1)} %bitcast.299), channel_id=1, source_target_pairs={{0,128},{128,256},{256,384},{1,129},{129,257},{257,385},{2,130},{1... | collective-permute-start | bytes 786440 | tf_op jit(solution)/shard_map/ppermute | solution.py:10
  305.8 9.3 %collective-permute-start.4 = (bf16[4,128,256]{2,0,1:T(4,128)(2,1)S(1)}, bf16[4,128,256]{2,0,1:T(4,128)(2,1)S(1)}, u32[]{:S(2)}, u32[]{:S(2)}) collective-permute-start(bf16[4,128,256]{2,0,1:T(4,128)(2,1)S(1)} %bitcast.300), channel_id=1, source_target_pairs={{0,128},{128,256},{256,384},{1,129},{129,257},{257,385},{2,130},{1... | collective-permute-start | bytes 786440 | tf_op jit(solution)/shard_map/ppermute | solution.py:10
  319.8 6.6 %copy-start.6 = (bf16[256]{0:T(256)(128)(2,1)S(1)}, bf16[256]{0:T(256)(128)(2,1)}, u32[]{:S(2)}) copy-start(bf16[256]{0:T(256)(128)(2,1)} %param.23) | copy-start | bytes 1540
  319.8 21.3 %all-to-all-start.10 = ((bf16[4,128,256]{2,0,1:T(4,128)(2,1)}), bf16[4,128,256]{2,0,1:T(4,128)(2,1)S(1)}, u32[]{:S(2)}, u32[]{:S(2)}) async-start(bf16[4,128,256]{2,0,1:T(4,128)(2,1)} %add_convert_fusion.1), calls=%async_computation.10 | async-start | bytes 524288 | tf_op jit(solution)/shard_map/all_to_all | solution.py:51
  345.3 21.5 %all-to-all-start.11 = ((bf16[128,2,512]{2,1,0:T(2,128)(2,1)}), bf16[128,2,512]{2,1,0:T(2,128)(2,1)S(1)}, u32[]{:S(2)}, u32[]{:S(2)}) async-start(bf16[128,2,512]{2,1,0:T(2,128)(2,1)} %reshape.1157), calls=%async_computation.11 | async-start | bytes 524288 | tf_op jit(solution)/shard_map/all_to_all | solution.py:66
  368.7 9.3 %collective-permute-start.5 = (bf16[4,128,256]{2,0,1:T(4,128)(2,1)S(1)}, bf16[4,128,256]{2,0,1:T(4,128)(2,1)S(1)}, u32[]{:S(2)}, u32[]{:S(2)}) collective-permute-start(bf16[4,128,256]{2,0,1:T(4,128)(2,1)S(1)} %bitcast.295), channel_id=1, source_target_pairs={{0,128},{128,256},{256,384},{1,129},{129,257},{257,385},{2,130},{1... | collective-permute-start | bytes 786440 | tf_op jit(solution)/shard_map/ppermute | solution.py:10
  382.7 21.1 %all-to-all-start.12 = ((bf16[4,128,256]{2,0,1:T(4,128)(2,1)}), bf16[4,128,256]{2,0,1:T(4,128)(2,1)S(1)}, u32[]{:S(2)}, u32[]{:S(2)}) async-start(bf16[4,128,256]{2,0,1:T(4,128)(2,1)} %add_convert_fusion), calls=%async_computation.12 | async-start | bytes 524288 | tf_op jit(solution)/shard_map/all_to_all | solution.py:51
  407.5 21.3 %all-to-all-start.13 = ((f32[4,512,1]{0,2,1:T(1,128)}), f32[4,512,1]{0,2,1:T(1,128)S(1)}, u32[]{:S(2)}, u32[]{:S(2)}) async-start(f32[4,512,1]{0,2,1:T(1,128)} %copy.117), calls=%async_computation.13 | async-start | bytes 524288 | tf_op jit(solution)/shard_map/all_to_all | solution.py:92
where the time goes:
time: 461 us; the launch traced here: 452 us
  blocking collectives  208 us (45%)
  waiting for transfers between devices  101 us (22%)
  starting transfers between devices  69.1 us (15%)
  other arithmetic  55 us (12%)
  local copies, waits for them, and re-layouts  11.5 us (2%)
  matrix products  5.43 us (1%)
    all_to_all x5, blocking collectives, to_rows(): lax.all_to_all(output, 'space', split_axis=0, concat_axis=1, tiled=True)  103 us
    all_to_all x4, blocking collectives, apply_layer(): lax.all_to_all(row_part, 'space', split_axis=1, concat_axis=0, tiled=True)  84.3 us
    all_to_all x3, waiting for transfers between devices, apply_layer(): lax.all_to_all(row_part, 'space', split_axis=1, concat_axis=0, tiled=True)  43.2 us
    all_to_all x3, starting transfers between devices, apply_layer(): lax.all_to_all(row_part, 'space', split_axis=1, concat_axis=0, tiled=True)  30.4 us
    ppermute x6, waiting for transfers between devices, from_behind(): return lax.ppermute(array, axis, pairs)  29.1 us
    convert_element_type x7, other arithmetic, apply_layer(): row_part = row_stencil(current, params[0]).astype(jnp.bfloat16)  26.7 us
    ppermute x6, starting transfers between devices, from_behind(): return lax.ppermute(array, axis, pairs)  25.4 us
    psum x1, blocking collectives, from_root(): return lax.psum(kept, axis)  20.7 us
  transfers between devices with their start and end apart: 11, of which 11 were waited for; matrix products, arithmetic and copies ran while one was open for 0% of the time, Pallas kernels for 0%

commit v1 on v0

v1 whole, which is shorter than its diff:
```python
import jax
import jax.numpy as jnp
from jax import lax
from jax.experimental import pallas as pl
from jax.experimental.pallas import tpu as pltpu
from jax.sharding import PartitionSpec as P

MESH = pl.DeviceIdType.MESH
F32, BF16 = jnp.float32, jnp.bfloat16
LAYERS, TAPS, RAD = 4, 15, 7
NY, NZ = 8, 8
ROWS = 8
HALF = 64
GROUP = 16
GROUPS = HALF // GROUP
CH, HID = 256, 512
BAND = 24 * GROUP


def remote(src, dst, send_sem, recv_sem, device):
    return pltpu.make_async_remote_copy(
        src_ref=src,
        dst_ref=dst,
        send_sem=send_sem,
        recv_sem=recv_sem,
        device_id=device,
        device_id_type=MESH,
    )


def kernel(
    raster, row_coef, col_coef, gain, w_in, bias, w_out, readout,
    out,
    S, R, A, LHS, WI, WO, RC, TT, CS, CT, ZS, ZB, YS, MC, MN, PB, DS, DR,
    lsem, zs, zr, ys, yr, xs, xr, rcs, rcr, ras, rar, pbs, pbr,
    ws, wr, fs, vs, vr, hs, hr, ss, sr, ds, dr,
):
    s = lax.axis_index("section")
    p = lax.axis_index("space")
    t, c = p // 2, p % 2
    y, z = t // NZ, t % NZ
    partner = (s, t * 2 + 1 - c)

    def sec(ds_):
        return lax.rem(s + ds_, LAYERS)

    def dev(yy, zz, cc):
        return (s, (yy * NZ + zz) * 2 + cc)

    prev_chip = (s, lax.rem(t + NY * NZ - 1, NY * NZ) * 2 + c)
    next_chip = (s, lax.rem(t + 1, NY * NZ) * 2 + c)

    barrier = pltpu.get_barrier_semaphore()
    greeted = []
    for k in range(1, LAYERS):
        greeted += [(sec(k), t * 2 + c), (sec(k), t * 2 + 1 - c)]
    for k in range(1, NZ):
        greeted.append(dev(y, lax.rem(z + k, NZ), c))
    for k in range(1, NY):
        for cc in range(2):
            greeted.append(dev(lax.rem(y + k, NY), z, cc))
    greeted += [partner, prev_chip, next_chip]
    for device in greeted:
        pl.semaphore_signal(barrier, inc=1, device_id=device, device_id_type=MESH)

    mine = pl.multiple_of(48 * c, 16)
    theirs = pl.multiple_of(48 * (1 - c), 16)
    mine_to = pl.multiple_of(16 - 16 * c, 16)
    theirs_to = pl.multiple_of(16 * c, 16)
    own_rows = pl.ds(c * 4, 4)
    loads = [
        pltpu.make_async_copy(
            raster.at[s, :, pl.ds(mine, 80), :],
            S.at[0, own_rows, pl.ds(mine_to, 80), :],
            lsem.at[0],
        ),
        pltpu.make_async_copy(w_in.at[0], WI.at[s], lsem.at[1]),
        pltpu.make_async_copy(w_out.at[0], WO.at[s], lsem.at[2]),
    ]
    for load in loads:
        load.start()

    edge = pl.multiple_of(80 * c, 16)
    for layer in range(LAYERS):
        S[layer, :, pl.ds(edge, 16), :] = jnp.zeros((ROWS, 16, CH), BF16)
        S[layer, :, 96:128, :] = jnp.zeros((ROWS, 32, CH), BF16)
        R[layer, :, 22:24] = jnp.zeros((GROUPS, 2, GROUP, CH), BF16)

        @pl.when(t == 0)
        def _():
            R[layer, :, 0:RAD] = jnp.zeros((GROUPS, RAD, GROUP, CH), BF16)

        @pl.when(t == NY * NZ - 1)
        def _():
            R[layer, :, 15:22] = jnp.zeros((GROUPS, RAD, GROUP, CH), BF16)

    rc = row_coef[0].astype(F32)
    for i in range(4):
        RC[s, c * 4 + i] = jnp.concatenate([rc[:, i, :], jnp.zeros((1, 128), F32)], axis=0)
    PB[s] = jnp.zeros((8, HID), F32)
    PB[s, 0:1, :] = bias[...].astype(F32)
    PB[s, 1:2, 0:CH] = gain[...].astype(F32)
    CS[...] = jnp.zeros(CS.shape, F32)
    CS[0:TAPS, :] = col_coef[0, :, 0, :].astype(F32)
    for q in range(4):
        CT[128 * q : 128 * (q + 1), :] = CS[:, 128 * q : 128 * (q + 1)].T
    for zz in range(NZ):
        total = CT[pl.ds(8 * zz, 8, stride=64), :]
        for r in range(1, ROWS):
            total = total + pltpu.roll(CT[pl.ds(8 * zz + r, 8, stride=64), :], 16 * r, 1)
        ZS[zz] = total

    pl.semaphore_wait(barrier, len(greeted))

    started = []

    def go(copy):
        copy.start()
        started.append(copy)

    for k in range(1, NZ):
        zz = lax.rem(z + k, NZ)
        go(remote(ZS.at[zz], ZB.at[z], zs.at[k], zr.at[k], dev(y, zz, c)))
    half = pl.ds(c * 4, 4)
    rows_sent = [(s, t * 2 + 1 - c)]
    for k in range(1, LAYERS):
        rows_sent += [(sec(k), t * 2 + c), (sec(k), t * 2 + 1 - c)]
    for k, device in enumerate(rows_sent):
        go(remote(RC.at[s, half], RC.at[s, half], rcs.at[k], rcr.at[s, c], device))
    go(
        remote(
            raster.at[s, :, pl.ds(theirs, 80), :],
            S.at[0, own_rows, pl.ds(theirs_to, 80), :],
            ras,
            rar,
            partner,
        )
    )
    for k in range(1, LAYERS):
        go(remote(PB.at[s], PB.at[s], pbs.at[k], pbr.at[s], (sec(k), p)))
    wi_half, wo_half = pl.ds(c * 128, 128), pl.ds(c * 256, 256)
    wi_other, wo_other = pl.ds((1 - c) * 128, 128), pl.ds((1 - c) * 256, 256)
    up, down = (sec(1), p), (sec(3), p)
    for k, device in enumerate((up, down)):
        go(remote(w_in.at[0, wi_half], WI.at[s, wi_half], ws.at[k, 0], wr.at[s, 0], device))
        go(remote(w_out.at[0, wo_half], WO.at[s, wo_half], ws.at[k, 1], wr.at[s, 1], device))

    def got_rows(layer):
        for h in range(2):

            @pl.when(jnp.logical_or(s != layer, c != h))
            def _():
                ref = RC.at[layer, pl.ds(4 * h, 4)]
                remote(ref, ref, rcs.at[0], rcr.at[layer, h], partner).wait_recv()

    lane = lax.broadcasted_iota(jnp.int32, (HALF, 128), 1)

    def build_rows(layer):
        TT[...] = RC[layer].reshape(128, 128).T
        taps = TT[pl.ds(pl.multiple_of(HALF * c, HALF), HALF), :]
        for i in range(ROWS):
            kept = jnp.where(lane // 16 == i, taps, 0.0)
            A[layer, i] = pltpu.roll(kept, (9 - 16 * i) % 128, 1, stride=1, stride_axis=0).astype(
                BF16
            )

    def row_stencil(layer):
        for i in range(ROWS):
            got = jnp.dot(A[layer, i], S[layer, i], preferred_element_type=F32).astype(BF16)
            for g in range(GROUPS):
                R[layer, g, RAD + i] = got[GROUP * g : GROUP * (g + 1)]

    def halo(layer, g, way):
        src, dst, device = ((7, 15, prev_chip), (8, 0, next_chip))[way]
        return remote(
            R.at[layer, g, pl.ds(src, RAD)],
            R.at[layer, g, pl.ds(dst, RAD)],
            hs.at[layer, way, g],
            hr.at[layer, way, g],
            device,
        )

    not_first, not_last = t > 0, t < NY * NZ - 1

    def order(step):
        return jnp.where(c == 0, GROUPS - 1 - step, step)

    def send_halos(layer):
        for step in range(GROUPS):
            g = order(step)

            @pl.when(not_first)
            def _():
                halo(layer, g, 0).start()

            @pl.when(not_last)
            def _():
                halo(layer, g, 1).start()

    def got_halos(layer, g):
        @pl.when(not_last)
        def _():
            halo(layer, g, 0).wait_recv()

        @pl.when(not_first)
        def _():
            halo(layer, g, 1).wait_recv()

    got_rows(0)
    build_rows(0)
    loads[0].wait()
    their_rows = pl.ds((1 - c) * 4, 4)
    remote(
        raster.at[s, :, pl.ds(theirs, 80), :],
        S.at[0, their_rows, pl.ds(mine_to, 80), :],
        ras,
        rar,
        partner,
    ).wait_recv()
    row_stencil(0)
    send_halos(0)

    ZB[z] = ZS[z]
    for k in range(1, NZ):
        remote(
            ZS.at[0], ZB.at[lax.rem(z + NZ - k, NZ)], zs.at[0], zr.at[k], partner
        ).wait_recv()
    d, gy = y // 4, y % 4
    for k in range(NY):
        yy = lax.rem(y + k, NY)
        YS[k] = ZB[pl.ds(0, NZ), yy, :]
        copy = remote(YS.at[k], MC.at[s, gy, c], ys.at[k], yr.at[gy, c], dev(yy, z, d))
        if k > 0:
            go(copy)
        else:

            @pl.when(d != c)
            def _():
                copy.start()

            @pl.when(d == c)
            def _():
                MC[s, gy, c] = YS[0]

            own_y = copy
    for l in range(1, LAYERS):
        got_rows(l)
        build_rows(l)
    for g in range(GROUPS):
        for cc in range(2):
            away = jnp.logical_or(jnp.logical_or(d != c, gy != g), c != cc)

            @pl.when(away)
            def _():
                remote(
                    YS.at[0], MC.at[s, g, cc], ys.at[0], yr.at[g, cc], partner
                ).wait_recv()

    for k in range(1, LAYERS):
        go(remote(MC.at[s], MC.at[s], xs.at[k], xr.at[s], (sec(k), p)))

    def weight_from(layer, piece):
        ref = (WI.at[layer, wi_half], WO.at[layer, wo_half])[piece]
        return remote(ref, ref, ws.at[0, 0], wr.at[layer, piece], partner)

    def pass_on(layer, piece, k):
        ref = (WI.at[layer, wi_half], WO.at[layer, wo_half])[piece]
        go(remote(ref, ref, vs.at[k, piece], vr.at[layer, piece], partner))

    below, above, across = sec(3), sec(1), sec(2)
    for piece in range(2):
        weight_from(below, piece).wait_recv()
        if piece == 0:
            ref = WI.at[below, wi_half]
            go(remote(ref, ref, fs.at[0], wr.at[below, 0], up))
        pass_on(below, piece, 0)
        weight_from(above, piece).wait_recv()
        if piece == 1:
            ref = WO.at[above, wo_half]
            go(remote(ref, ref, fs.at[1], wr.at[above, 1], down))
        pass_on(above, piece, 1)
    for piece in range(2):
        weight_from(across, piece).wait_recv()
        pass_on(across, piece, 2)
    for load in loads[1:]:
        load.wait()

    row_id = lax.broadcasted_iota(jnp.int32, (128, 256), 0)
    lane_id = lax.broadcasted_iota(jnp.int32, (128, 256), 1)
    spread = jnp.where(row_id == lane_id // 16, 1.0, 0.0).astype(BF16)
    spread = jnp.where(row_id < 16, spread, jnp.zeros_like(spread))
    diag = (
        lax.broadcasted_iota(jnp.int32, (HALF, 256), 1) % 16
        == lax.broadcasted_iota(jnp.int32, (HALF, 256), 0) % 16
    )

    def got_cols(layer):
        @pl.when(s != layer)
        def _():
            remote(MC.at[layer], MC.at[layer], xs.at[0], xr.at[layer], partner).wait_recv()
            remote(PB.at[layer], PB.at[layer], pbs.at[0], pbr.at[layer], partner).wait_recv()
            for piece in range(2):
                ref = (WI.at[layer, wi_other], WO.at[layer, wo_other])[piece]
                remote(ref, ref, vs.at[0, 0], vr.at[layer, piece], partner).wait_recv()

    def build_cols(layer):
        for g in range(GROUPS):
            for cc in range(2):
                MN[pl.ds(GROUP * g + cc, 8, stride=2), :] = MC[layer, g, cc]
        taps = MN[...]
        for i in range(ROWS):
            turned = taps if i == 0 else pltpu.roll(taps, 128 - 16 * i, 1)
            wide = jnp.dot(turned.astype(BF16), spread, preferred_element_type=F32)
            wide = jnp.where(diag, wide, 0.0)
            wide = jnp.concatenate([wide, jnp.zeros((HALF, 128), F32)], axis=1)
            if i:
                wide = pltpu.roll(wide, 16 * i, 1)
            wide = wide.astype(BF16)
            for g in range(GROUPS):
                LHS[layer, g, GROUP * i : GROUP * (i + 1), :] = wide[GROUP * g : GROUP * (g + 1)]

    def dense(layer, g):
        field = jnp.dot(
            LHS[layer, g], R[layer, g].reshape(BAND, CH), preferred_element_type=F32
        )
        inverse = lax.rsqrt(jnp.mean(field * field, axis=-1, keepdims=True) + 1e-06)
        normed = (field * inverse * PB[layer, 1:2, 0:CH]).astype(BF16)
        hidden = jax.nn.gelu(
            jnp.dot(normed, WI[layer], preferred_element_type=F32) + PB[layer, 0:1, :],
            approximate=True,
        ).astype(BF16)
        state = (field + jnp.dot(hidden, WO[layer], preferred_element_type=F32)).astype(BF16)
        at = pl.ds(pl.multiple_of(16 + GROUP * g, 16), GROUP)
        for i in range(ROWS):
            S[layer + 1, i, at, :] = state[GROUP * i : GROUP * (i + 1)]

    edge_from = pl.multiple_of(64 - 48 * c, 16)
    edge_to = pl.multiple_of(80 * c, 16)
    edge_in = pl.multiple_of(80 - 80 * c, 16)

    def edge_copy(layer):
        return remote(
            S.at[layer, :, pl.ds(edge_from, 16), :],
            S.at[layer, :, pl.ds(edge_to, 16), :],
            ss.at[layer],
            sr.at[layer],
            partner,
        )

    for layer in range(LAYERS):
        if layer > 0:
            ref = S.at[layer, :, pl.ds(edge_in, 16), :]
            remote(ref, ref, ss.at[layer], sr.at[layer], partner).wait_recv()
            row_stencil(layer)
            send_halos(layer)
        got_cols(layer)
        build_cols(layer)
        for step in range(GROUPS):
            g = order(step)
            got_halos(layer, g)
            dense(layer, g)
            if step == 0 and layer < LAYERS - 1:
                go(edge_copy(layer + 1))

    weights = jnp.broadcast_to(readout[...].astype(F32), (8, CH))
    which = lax.broadcasted_iota(jnp.int32, (8, CH), 0)
    logits = jnp.zeros((8, HALF), F32)
    for i in range(ROWS):
        logits = logits + lax.dot_general(
            jnp.where(which == i, weights, 0.0).astype(BF16),
            S[LAYERS, i, 16 : 16 + HALF, :],
            (((1,), (1,)), ((), ())),
            preferred_element_type=F32,
        )
    values = jax.nn.softplus(jnp.concatenate([logits, logits], axis=1))
    DS[0] = values
    DS[1] = pltpu.roll(values, 4, 0)
    go(remote(DS.at[1 - c], DR, ds, dr, partner))
    remote(DS.at[c], DR, ds, dr, partner).wait_recv()
    cols = lax.broadcasted_iota(jnp.int32, (8, 128), 1)
    out[0] = jnp.where(cols // HALF == c, DS[c], DR[...])[0:4]

    for copy in started:
        copy.wait_send()

    @pl.when(d != c)
    def _():
        own_y.wait_send()

    for layer in range(LAYERS):
        for g in range(GROUPS):

            @pl.when(not_first)
            def _():
                halo(layer, g, 0).wait_send()

            @pl.when(not_last)
            def _():
                halo(layer, g, 1).wait_send()


def on_device(raster, row_coef, col_coef, norm_gain, weight_in, bias_in, weight_out, readout):
    vmem = pl.BlockSpec(memory_space=pltpu.VMEM)
    anywhere = pl.BlockSpec(memory_space=pl.ANY)
    dma = pltpu.SemaphoreType.DMA
    return pl.pallas_call(
        kernel,
        out_shape=jax.ShapeDtypeStruct((1, 4, 128), F32),
        in_specs=[anywhere, vmem, vmem, vmem, anywhere, vmem, anywhere, vmem],
        out_specs=vmem,
        scratch_shapes=[
            pltpu.VMEM((LAYERS + 1, ROWS, 128, CH), BF16),
            pltpu.VMEM((LAYERS, GROUPS, 24, GROUP, CH), BF16),
            pltpu.VMEM((LAYERS, ROWS, HALF, 128), BF16),
            pltpu.VMEM((LAYERS, GROUPS, 128, BAND), BF16),
            pltpu.VMEM((LAYERS, CH, HID), BF16),
            pltpu.VMEM((LAYERS, HID, CH), BF16),
            pltpu.VMEM((LAYERS, ROWS, 16, 128), F32),
            pltpu.VMEM((128, 128), F32),
            pltpu.VMEM((128, 512), F32),
            pltpu.VMEM((512, 128), F32),
            pltpu.VMEM((NZ, 8, 128), F32),
            pltpu.VMEM((NZ, 8, 128), F32),
            pltpu.VMEM((NY, 8, 128), F32),
            pltpu.VMEM((LAYERS, GROUPS, 2, 8, 128), F32),
            pltpu.VMEM((HALF, 128), F32),
            pltpu.VMEM((LAYERS, 8, HID), F32),
            pltpu.VMEM((2, 8, 128), F32),
            pltpu.VMEM((8, 128), F32),
            dma((3,)),
            dma((NZ,)), dma((NZ,)),
            dma((NY,)), dma((GROUPS, 2)),
            dma((LAYERS,)), dma((LAYERS,)),
            dma((7,)), dma((LAYERS, 2)),
            dma, dma,
            dma((LAYERS,)), dma((LAYERS,)),
            dma((2, 2)), dma((LAYERS, 2)), dma((2,)),
            dma((3, 2)), dma((LAYERS, 2)),
            dma((LAYERS, 2, GROUPS)), dma((LAYERS, 2, GROUPS)),
            dma((LAYERS,)), dma((LAYERS,)),
            dma, dma,
        ],
        compiler_params=pltpu.CompilerParams(
            collective_id=0, has_side_effects=True, vmem_limit_bytes=48 * 1024 * 1024
        ),
        name="forecast",
    )(
        raster, row_coef, col_coef, norm_gain, weight_in, bias_in, weight_out,
        readout.reshape(1, CH),
    )


def solution(mesh):
    placed = (
        P(None, "space", None, None),
        P("section", None, "space", None),
        P("section", None, "space", None),
        P("section", None),
        P("section", None, None),
        P("section", None),
        P("section", None, None),
        P(),
    )
    return jax.shard_map(
        on_device,
        mesh=mesh,
        in_specs=placed,
        out_specs=P("section", "space", None),
        check_vma=False,
    )
```

time: 461 us -> 70.7 us (0.15); the launches traced: 452 us -> 69.8 us
  blocking collectives: 208 us -> 0 us
  waiting for transfers between devices: 101 us -> 0 us
  starting transfers between devices: 69.1 us -> 0 us
  Pallas kernels: 0 us -> 64.6 us
  other arithmetic: 55 us -> 0 us
  local copies, waits for them, and re-layouts: 11.5 us -> 5.15 us
  matrix products: 5.43 us -> 0 us
    all_to_all x9 -> x0, blocking collectives: 188 us -> none  [the longest x5 103 us: to_rows(): lax.all_to_all(output, 'space', split_axis=0, concat_axis=1, tiled=True)]
    all_to_all x5 -> x0, waiting for transfers between devices: 72.3 us -> none  [the longest x3 43.2 us: apply_layer(): lax.all_to_all(row_part, 'space', split_axis=1, concat_axis=0, tiled=True)]
    pallas_call x0 -> x1, Pallas kernels: none -> 64.6 us  [on_device(): pl.pallas_call(kernel, out_shape=jax.ShapeDtypeStruct((1, 4, 128), F32),...]
    all_to_all x5 -> x0, starting transfers between devices: 43.7 us -> none  [the longest x3 30.4 us: apply_layer(): lax.all_to_all(row_part, 'space', split_axis=1, concat_axis=0, tiled=True)]
    convert_element_type x31 -> x0, other arithmetic: 33.6 us -> none  [the longest x7 26.7 us: apply_layer(): row_part = row_stencil(current, params[0]).astype(jnp.bfloat16)]
    ppermute x6 -> x0, waiting for transfers between devices: 29.1 us -> none  [from_behind(): return lax.ppermute(array, axis, pairs)]
    ppermute x6 -> x0, starting transfers between devices: 25.4 us -> none  [from_behind(): return lax.ppermute(array, axis, pairs)]
    psum x1 -> x0, blocking collectives: 20.7 us -> none  [from_root(): return lax.psum(kept, axis)]
  transfers between devices with their start and end apart: 11 -> 0, of which waited for: 11 -> 0; matrix products, arithmetic and copies ran while one was open for 0% -> 0% of each run, Pallas kernels for 0% -> 0%
where the time goes in v1:
time: 70.7 us; the launch traced here: 69.8 us
  Pallas kernels  64.6 us (91%)
  local copies, waits for them, and re-layouts  5.15 us (7%)
    pallas_call x1, Pallas kernels, on_device(): pl.pallas_call(kernel, out_shape=jax.ShapeDtypeStruct((1, 4, 128), F32),...  64.6 us
    unnamed x14, local copies, waits for them, and re-layouts  4.49 us

profile of v1, /device:TPU:8, one launch (start us, length us, event | category | flops | bytes accessed | tf_op | source)
XLA Modules:
  0.0 69.8 jit_solution(13533572171765646139)
XLA Ops:
  0.0 0.7 reshape.3.readout
  0.7 0.0 copy-start.3
  0.7 0.0 copy-start.4
  0.7 0.0 copy-start.5
  0.7 0.8 %copy.9.col_coef = bf16[1,15,1,512]{3,2,1,0:T(2,128)(2,1)S(1)} copy(bf16[1,15,1,512]{3,1,2,0:T(8,128)(2,1)} %param.10) | data formatting | bytes 30720 | tf_op args[2]
  1.5 0.0 copy-done.3
  1.5 0.0 copy-done.4
  1.5 0.0 copy-done.5
  1.5 0.0 copy-start
  1.5 1.2 %copy-done = bf16[4,4,128,256]{3,2,1,0:T(8,128)(2,1)S(1)} copy-done((bf16[4,4,128,256]{3,2,1,0:T(8,128)(2,1)S(1)}, bf16[4,4,128,256]{3,2,1,0:T(8,128)(2,1)}, u32[]{:S(2)}) %copy-start) | copy-done | bytes 1048600
  2.7 0.0 copy-start.1
  2.7 0.9 %copy-done.1 = bf16[1,256,512]{2,1,0:T(8,128)(2,1)S(1)} copy-done((bf16[1,256,512]{2,1,0:T(8,128)(2,1)S(1)}, bf16[1,256,512]{2,1,0:T(8,128)(2,1)}, u32[]{:S(2)}) %copy-start.1) | copy-done | bytes 262168
  3.7 0.0 copy-start.2
  3.7 0.9 %copy-done.2 = bf16[1,512,256]{2,1,0:T(8,128)(2,1)S(1)} copy-done((bf16[1,512,256]{2,1,0:T(8,128)(2,1)S(1)}, bf16[1,512,256]{2,1,0:T(8,128)(2,1)}, u32[]{:S(2)}) %copy-start.2) | copy-done | bytes 262168
  4.6 64.6 %forecast.1 = f32[1,4,128]{2,1,0:T(4,128)S(1)} custom-call(bf16[4,4,128,256]{3,2,1,0:T(8,128)(2,1)S(1)} %copy-done, bf16[1,15,4,128]{3,2,1,0:T(4,128)(2,1)S(1)} %copy-done.3, bf16[1,15,1,512]{3,2,1,0:T(2,128)(2,1)S(1)} %copy.9.col_coef, bf16[1,256]{1,0:T(2,128)(2,1)S(1)} %copy-done.5, bf16[1,256,512]{2,1,0:T(8,128)(2,1)S(1)} %copy-done.1, ...), custom_call_target="tpu_custom_call" | custom-call | tf_op jit(solution)/shard_map/forecast/pallas_call | solution.py:406
  69.2 0.6 copy.11
Async XLA Ops:
  0.7 0.8 %copy-start.3 = (bf16[1,15,4,128]{3,2,1,0:T(4,128)(2,1)S(1)}, bf16[1,15,4,128]{3,2,1,0:T(4,128)(2,1)}, u32[]{:S(2)}) copy-start(bf16[1,15,4,128]{3,2,1,0:T(4,128)(2,1)} %row_coef.1) | copy-start | bytes 46084
  0.7 0.8 %copy-start.4 = (bf16[1,512]{1,0:T(2,128)(2,1)S(1)}, bf16[1,512]{1,0:T(2,128)(2,1)}, u32[]{:S(2)}) copy-start(bf16[1,512]{1,0:T(2,128)(2,1)} %bias.1) | copy-start | bytes 3076
  0.7 0.8 %copy-start.5 = (bf16[1,256]{1,0:T(2,128)(2,1)S(1)}, bf16[1,256]{1,0:T(2,128)(2,1)}, u32[]{:S(2)}) copy-start(bf16[1,256]{1,0:T(2,128)(2,1)} %gain.1) | copy-start | bytes 1540
  1.5 1.2 %copy-start = (bf16[4,4,128,256]{3,2,1,0:T(8,128)(2,1)S(1)}, bf16[4,4,128,256]{3,2,1,0:T(8,128)(2,1)}, u32[]{:S(2)}) copy-start(bf16[4,4,128,256]{3,2,1,0:T(8,128)(2,1)} %raster.1) | copy-start | bytes 3145732
  2.7 0.9 %copy-start.1 = (bf16[1,256,512]{2,1,0:T(8,128)(2,1)S(1)}, bf16[1,256,512]{2,1,0:T(8,128)(2,1)}, u32[]{:S(2)}) copy-start(bf16[1,256,512]{2,1,0:T(8,128)(2,1)} %w_in.1) | copy-start | bytes 786436
  3.7 0.9 %copy-start.2 = (bf16[1,512,256]{2,1,0:T(8,128)(2,1)S(1)}, bf16[1,512,256]{2,1,0:T(8,128)(2,1)}, u32[]{:S(2)}) copy-start(bf16[1,512,256]{2,1,0:T(8,128)(2,1)} %w_out.1) | copy-start | bytes 786436

commit v2 on v1

--- a/solution.py
+++ b/solution.py
@@ -32,7 +32,7 @@
     raster, row_coef, col_coef, gain, w_in, bias, w_out, readout,
     out,
     S, R, A, LHS, WI, WO, RC, TT, CS, CT, ZS, ZB, YS, MC, MN, PB, DS, DR,
-    lsem, zs, zr, ys, yr, xs, xr, rcs, rcr, ras, rar, pbs, pbr,
+    lsem, zs, zr, ys, yr, rcs, rcr, ras, rar, pbs, pbr,
     ws, wr, fs, vs, vr, hs, hr, ss, sr, ds, dr,
 ):
     s = lax.axis_index("section")
@@ -52,13 +52,14 @@
 
     barrier = pltpu.get_barrier_semaphore()
     greeted = []
-    for k in range(1, LAYERS):
-        greeted += [(sec(k), t * 2 + c), (sec(k), t * 2 + 1 - c)]
+    for k in range(LAYERS):
+        for j in range(NY):
+            yy = lax.rem(y + j, NY)
+            for cc in range(2):
+                if k or j:
+                    greeted.append((sec(k), (yy * NZ + z) * 2 + (c + cc) % 2))
     for k in range(1, NZ):
         greeted.append(dev(y, lax.rem(z + k, NZ), c))
-    for k in range(1, NY):
-        for cc in range(2):
-            greeted.append(dev(lax.rem(y + k, NY), z, cc))
     greeted += [partner, prev_chip, next_chip]
     for device in greeted:
         pl.semaphore_signal(barrier, inc=1, device_id=device, device_id_type=MESH)
@@ -83,7 +84,6 @@
     edge = pl.multiple_of(80 * c, 16)
     for layer in range(LAYERS):
         S[layer, :, pl.ds(edge, 16), :] = jnp.zeros((ROWS, 16, CH), BF16)
-        S[layer, :, 96:128, :] = jnp.zeros((ROWS, 32, CH), BF16)
         R[layer, :, 22:24] = jnp.zeros((GROUPS, 2, GROUP, CH), BF16)
 
         @pl.when(t == 0)
@@ -101,7 +101,7 @@
     PB[s, 0:1, :] = bias[...].astype(F32)
     PB[s, 1:2, 0:CH] = gain[...].astype(F32)
     CS[...] = jnp.zeros(CS.shape, F32)
-    CS[0:TAPS, :] = col_coef[0, :, 0, :].astype(F32)
+    CS[0:TAPS, :] = col_coef[0, 0].astype(F32)
     for q in range(4):
         CT[128 * q : 128 * (q + 1), :] = CS[:, 128 * q : 128 * (q + 1)].T
     for zz in range(NZ):
@@ -142,8 +142,10 @@
     wi_other, wo_other = pl.ds((1 - c) * 128, 128), pl.ds((1 - c) * 256, 256)
     up, down = (sec(1), p), (sec(3), p)
     for k, device in enumerate((up, down)):
-        go(remote(w_in.at[0, wi_half], WI.at[s, wi_half], ws.at[k, 0], wr.at[s, 0], device))
-        go(remote(w_out.at[0, wo_half], WO.at[s, wo_half], ws.at[k, 1], wr.at[s, 1], device))
+        for piece in (k, 1 - k):
+            src = (w_in.at[0, wi_half], w_out.at[0, wo_half])[piece]
+            dst = (WI.at[s, wi_half], WO.at[s, wo_half])[piece]
+            go(remote(src, dst, ws.at[k, piece], wr.at[s, piece], device))
 
     def got_rows(layer):
         for h in range(2):
@@ -160,15 +162,23 @@
         taps = TT[pl.ds(pl.multiple_of(HALF * c, HALF), HALF), :]
         for i in range(ROWS):
             kept = jnp.where(lane // 16 == i, taps, 0.0)
-            A[layer, i] = pltpu.roll(kept, (9 - 16 * i) % 128, 1, stride=1, stride_axis=0).astype(
-                BF16
-            )
-
-    def row_stencil(layer):
+            for g in range(GROUPS):
+                A[layer, g, i] = pltpu.roll(
+                    kept[GROUP * g : GROUP * (g + 1)],
+                    (9 - 16 * i) % 128,
+                    1,
+                    stride=1,
+                    stride_axis=0,
+                ).astype(BF16)
+
+    def row_stencil(layer, g):
+        window = pl.ds(pl.multiple_of(GROUP * g, GROUP), 3 * GROUP)
         for i in range(ROWS):
-            got = jnp.dot(A[layer, i], S[layer, i], preferred_element_type=F32).astype(BF16)
-            for g in range(GROUPS):
-                R[layer, g, RAD + i] = got[GROUP * g : GROUP * (g + 1)]
+            R[layer, g, RAD + i] = jnp.dot(
+                A[layer, g, i][:, 0 : 3 * GROUP],
+                S[layer, i, window, :],
+                preferred_element_type=F32,
+            ).astype(BF16)
 
     def halo(layer, g, way):
         src, dst, device = ((7, 15, prev_chip), (8, 0, next_chip))[way]
@@ -183,19 +193,18 @@
     not_first, not_last = t > 0, t < NY * NZ - 1
 
     def order(step):
-        return jnp.where(c == 0, GROUPS - 1 - step, step)
-
-    def send_halos(layer):
-        for step in range(GROUPS):
-            g = order(step)
-
-            @pl.when(not_first)
-            def _():
-                halo(layer, g, 0).start()
-
-            @pl.when(not_last)
-            def _():
-                halo(layer, g, 1).start()
+        return jnp.where(c == 0, step, GROUPS - 1 - step)
+
+    def send_row(layer, g):
+        row_stencil(layer, g)
+
+        @pl.when(not_first)
+        def _():
+            halo(layer, g, 0).start()
+
+        @pl.when(not_last)
+        def _():
+            halo(layer, g, 1).start()
 
     def got_halos(layer, g):
         @pl.when(not_last)
@@ -217,8 +226,8 @@
         rar,
         partner,
     ).wait_recv()
-    row_stencil(0)
-    send_halos(0)
+    for step in range(GROUPS):
+        send_row(0, order(step))
 
     ZB[z] = ZS[z]
     for k in range(1, NZ):
@@ -226,59 +235,57 @@
             ZS.at[0], ZB.at[lax.rem(z + NZ - k, NZ)], zs.at[0], zr.at[k], partner
         ).wait_recv()
     d, gy = y // 4, y % 4
-    for k in range(NY):
-        yy = lax.rem(y + k, NY)
-        YS[k] = ZB[pl.ds(0, NZ), yy, :]
-        copy = remote(YS.at[k], MC.at[s, gy, c], ys.at[k], yr.at[gy, c], dev(yy, z, d))
-        if k > 0:
-            go(copy)
-        else:
-
-            @pl.when(d != c)
-            def _():
-                copy.start()
-
-            @pl.when(d == c)
-            def _():
-                MC[s, gy, c] = YS[0]
-
-            own_y = copy
+    for j in range(NY):
+        yy = lax.rem(y + j, NY)
+        YS[j] = ZB[pl.ds(0, NZ), yy, :]
+    for k in range(LAYERS):
+        for j in range(NY):
+            yy = lax.rem(y + j, NY)
+            copy = remote(
+                YS.at[j],
+                MC.at[s, gy, c],
+                ys.at[k, j],
+                yr.at[s, gy, c],
+                (sec(k), (yy * NZ + z) * 2 + d),
+            )
+            if k or j:
+                go(copy)
+            else:
+
+                @pl.when(d != c)
+                def _():
+                    copy.start()
+
+                @pl.when(d == c)
+                def _():
+                    MC[s, gy, c] = YS[0]
+
+                own_y = copy
+
+    def weight_from(layer, piece):
+        ref = (WI.at[layer, wi_half], WO.at[layer, wo_half])[piece]
+        return remote(ref, ref, ws.at[0, 0], wr.at[layer, piece], partner)
+
+    def pass_on(layer, piece, k):
+        ref = (WI.at[layer, wi_half], WO.at[layer, wo_half])[piece]
+        go(remote(ref, ref, vs.at[k, piece], vr.at[layer, piece], partner))
+
+    below, above, across = sec(3), sec(1), sec(2)
+    weight_from(below, 0).wait_recv()
+    ref = WI.at[below, wi_half]
+    go(remote(ref, ref, fs.at[0], wr.at[below, 0], up))
+    weight_from(above, 1).wait_recv()
+    ref = WO.at[above, wo_half]
+    go(remote(ref, ref, fs.at[1], wr.at[above, 1], down))
+    pass_on(below, 0, 0)
+    pass_on(above, 1, 1)
+    weight_from(below, 1).wait_recv()
+    pass_on(below, 1, 0)
+    weight_from(above, 0).wait_recv()
+    pass_on(above, 0, 1)
     for l in range(1, LAYERS):
         got_rows(l)
         build_rows(l)
-    for g in range(GROUPS):
-        for cc in range(2):
-            away = jnp.logical_or(jnp.logical_or(d != c, gy != g), c != cc)
-
-            @pl.when(away)
-            def _():
-                remote(
-                    YS.at[0], MC.at[s, g, cc], ys.at[0], yr.at[g, cc], partner
-                ).wait_recv()
-
-    for k in range(1, LAYERS):
-        go(remote(MC.at[s], MC.at[s], xs.at[k], xr.at[s], (sec(k), p)))
-
-    def weight_from(layer, piece):
-        ref = (WI.at[layer, wi_half], WO.at[layer, wo_half])[piece]
-        return remote(ref, ref, ws.at[0, 0], wr.at[layer, piece], partner)
-
-    def pass_on(layer, piece, k):
-        ref = (WI.at[layer, wi_half], WO.at[layer, wo_half])[piece]
-        go(remote(ref, ref, vs.at[k, piece], vr.at[layer, piece], partner))
-
-    below, above, across = sec(3), sec(1), sec(2)
-    for piece in range(2):
-        weight_from(below, piece).wait_recv()
-        if piece == 0:
-            ref = WI.at[below, wi_half]
-            go(remote(ref, ref, fs.at[0], wr.at[below, 0], up))
-        pass_on(below, piece, 0)
-        weight_from(above, piece).wait_recv()
-        if piece == 1:
-            ref = WO.at[above, wo_half]
-            go(remote(ref, ref, fs.at[1], wr.at[above, 1], down))
-        pass_on(above, piece, 1)
     for piece in range(2):
         weight_from(across, piece).wait_recv()
         pass_on(across, piece, 2)
@@ -295,9 +302,19 @@
     )
 
     def got_cols(layer):
+        for g in range(GROUPS):
+            for cc in range(2):
+                here = jnp.logical_and(s == layer, jnp.logical_and(d == c, gy == g))
+
+                @pl.when(jnp.logical_not(jnp.logical_and(here, c == cc)))
+                def _():
+                    remote(
+                        YS.at[0], MC.at[layer, g, cc], ys.at[0, 0], yr.at[layer, g, cc], partner
+                    ).wait_recv()
+
+    def got_weights(layer):
         @pl.when(s != layer)
         def _():
-            remote(MC.at[layer], MC.at[layer], xs.at[0], xr.at[layer], partner).wait_recv()
             remote(PB.at[layer], PB.at[layer], pbs.at[0], pbr.at[layer], partner).wait_recv()
             for piece in range(2):
                 ref = (WI.at[layer, wi_other], WO.at[layer, wo_other])[piece]
@@ -347,22 +364,28 @@
             partner,
         )
 
+    got_cols(0)
+    build_cols(0)
     for layer in range(LAYERS):
         if layer > 0:
             ref = S.at[layer, :, pl.ds(edge_in, 16), :]
             remote(ref, ref, ss.at[layer], sr.at[layer], partner).wait_recv()
-            row_stencil(layer)
-            send_halos(layer)
-        got_cols(layer)
-        build_cols(layer)
+            send_row(layer, order(GROUPS - 1))
+        got_weights(layer)
+        if layer + 1 < LAYERS:
+            got_cols(layer + 1)
+            build_cols(layer + 1)
         for step in range(GROUPS):
             g = order(step)
             got_halos(layer, g)
             dense(layer, g)
-            if step == 0 and layer < LAYERS - 1:
-                go(edge_copy(layer + 1))
-
-    weights = jnp.broadcast_to(readout[...].astype(F32), (8, CH))
+            if layer + 1 < LAYERS:
+                if step == GROUPS - 1:
+                    go(edge_copy(layer + 1))
+                if step > 0:
+                    send_row(layer + 1, order(step - 1))
+
+    weights = jnp.broadcast_to(readout[...].astype(F32).reshape(1, CH), (8, CH))
     which = lax.broadcasted_iota(jnp.int32, (8, CH), 0)
     logits = jnp.zeros((8, HALF), F32)
     for i in range(ROWS):
@@ -409,9 +432,9 @@
         in_specs=[anywhere, vmem, vmem, vmem, anywhere, vmem, anywhere, vmem],
         out_specs=vmem,
         scratch_shapes=[
-            pltpu.VMEM((LAYERS + 1, ROWS, 128, CH), BF16),
+            pltpu.VMEM((LAYERS + 1, ROWS, 96, CH), BF16),
             pltpu.VMEM((LAYERS, GROUPS, 24, GROUP, CH), BF16),
-            pltpu.VMEM((LAYERS, ROWS, HALF, 128), BF16),
+            pltpu.VMEM((LAYERS, GROUPS, ROWS, GROUP, 128), BF16),
             pltpu.VMEM((LAYERS, GROUPS, 128, BAND), BF16),
             pltpu.VMEM((LAYERS, CH, HID), BF16),
             pltpu.VMEM((LAYERS, HID, CH), BF16),
@@ -429,8 +452,7 @@
             pltpu.VMEM((8, 128), F32),
             dma((3,)),
             dma((NZ,)), dma((NZ,)),
-            dma((NY,)), dma((GROUPS, 2)),
-            dma((LAYERS,)), dma((LAYERS,)),
+            dma((LAYERS, NY)), dma((LAYERS, GROUPS, 2)),
             dma((7,)), dma((LAYERS, 2)),
             dma, dma,
             dma((LAYERS,)), dma((LAYERS,)),
@@ -441,12 +463,12 @@
             dma, dma,
         ],
         compiler_params=pltpu.CompilerParams(
-            collective_id=0, has_side_effects=True, vmem_limit_bytes=48 * 1024 * 1024
+            collective_id=0, has_side_effects=True, vmem_limit_bytes=67043328
         ),
         name="forecast",
     )(
-        raster, row_coef, col_coef, norm_gain, weight_in, bias_in, weight_out,
-        readout.reshape(1, CH),
+        raster, row_coef, jnp.swapaxes(col_coef, 1, 2), norm_gain, weight_in, bias_in, weight_out,
+        readout,
     )
 
 

time: 70.7 us -> 60.9 us (0.86)
  the two profiles are of different devices: /device:TPU:8 before, /device:TPU:15 now
where the time goes in v2:
time: 60.9 us; the launch traced here: 60.7 us
  Pallas kernels  59.5 us (98%)
  local copies, waits for them, and re-layouts  1.26 us (2%)
    pallas_call x1, Pallas kernels, on_device(): pl.pallas_call(kernel, out_shape=jax.ShapeDtypeStruct((1, 4, 128), F32),...  59.5 us
    unnamed x1, local copies, waits for them, and re-layouts  1.26 us

profile of v2, /device:TPU:15, one launch (start us, length us, event | category | flops | bytes accessed | tf_op | source)
XLA Modules:
  0.0 60.7 jit_solution(10634789347992807810)
XLA Ops:
  0.0 59.5 %forecast.1 = f32[1,4,128]{2,1,0:T(4,128)} custom-call(bf16[4,4,128,256]{3,2,1,0:T(8,128)(2,1)} %raster.1, bf16[1,15,4,128]{3,2,1,0:T(4,128)(2,1)} %row_coef.1, bf16[1,1,15,512]{3,2,1,0:T(8,128)(2,1)} %bitcast.1, bf16[1,256]{1,0:T(2,128)(2,1)} %gain.1, bf16[1,256,512]{2,1,0:T(8,128)(2,1)} %w_in.1, bf16[1,512]{1,0:T(2,128)(2,1)} %bias.1, ...), custom_call_target="tpu_custom_call" | custom-call | tf_op jit(solution)/shard_map/forecast/pallas_call | solution.py:429
  59.5 1.3 %copy.10 = f32[1,4,128]{2,1,0:T(4,128)} copy(f32[1,4,128]{2,1,0:T(4,128)} %forecast.1) | data formatting | bytes 4096

commit v3 on v2

--- a/solution.py
+++ b/solution.py
@@ -31,7 +31,7 @@
 def kernel(
     raster, row_coef, col_coef, gain, w_in, bias, w_out, readout,
     out,
-    S, R, A, LHS, WI, WO, RC, TT, CS, CT, ZS, ZB, YS, MC, MN, PB, DS, DR,
+    rcv, ccv, gv, bv, rv, S, R, A, LHS, WI, WO, RC, TT, CS, CT, ZS, ZB, YS, MC, MN, PB, DS, DR,
     lsem, zs, zr, ys, yr, rcs, rcr, ras, rar, pbs, pbr,
     ws, wr, fs, vs, vr, hs, hr, ss, sr, ds, dr,
 ):
@@ -50,58 +50,56 @@
     prev_chip = (s, lax.rem(t + NY * NZ - 1, NY * NZ) * 2 + c)
     next_chip = (s, lax.rem(t + 1, NY * NZ) * 2 + c)
 
-    barrier = pltpu.get_barrier_semaphore()
-    greeted = []
-    for k in range(LAYERS):
-        for j in range(NY):
-            yy = lax.rem(y + j, NY)
-            for cc in range(2):
-                if k or j:
-                    greeted.append((sec(k), (yy * NZ + z) * 2 + (c + cc) % 2))
-    for k in range(1, NZ):
-        greeted.append(dev(y, lax.rem(z + k, NZ), c))
-    greeted += [partner, prev_chip, next_chip]
-    for device in greeted:
-        pl.semaphore_signal(barrier, inc=1, device_id=device, device_id_type=MESH)
-
+    d, gy = y // 4, y % 4
     mine = pl.multiple_of(48 * c, 16)
     theirs = pl.multiple_of(48 * (1 - c), 16)
     mine_to = pl.multiple_of(16 - 16 * c, 16)
     theirs_to = pl.multiple_of(16 * c, 16)
     own_rows = pl.ds(c * 4, 4)
+    small = [
+        pltpu.make_async_copy(src, dst, lsem.at[k])
+        for k, (src, dst) in enumerate(
+            ((col_coef.at[0, 0], ccv), (row_coef.at[0], rcv), (gain, gv), (bias, bv), (readout, rv))
+        )
+    ]
     loads = [
         pltpu.make_async_copy(
             raster.at[s, :, pl.ds(mine, 80), :],
             S.at[0, own_rows, pl.ds(mine_to, 80), :],
-            lsem.at[0],
+            lsem.at[5],
         ),
-        pltpu.make_async_copy(w_in.at[0], WI.at[s], lsem.at[1]),
-        pltpu.make_async_copy(w_out.at[0], WO.at[s], lsem.at[2]),
+        pltpu.make_async_copy(w_in.at[0], WI.at[s], lsem.at[6]),
+        pltpu.make_async_copy(w_out.at[0], WO.at[s], lsem.at[7]),
     ]
+    for load in small:
+        load.start()
+
+    barrier = pltpu.get_barrier_semaphore()
+    greeted = []
+    for k in range(LAYERS):
+        for j in range(4):
+            for cc in range(2):
+                greeted.append((sec(k), ((c * 4 + (y + j) % 4) * NZ + z) * 2 + (c + cc) % 2))
+    for k in range(1, NZ):
+        greeted.append(dev(y, lax.rem(z + k, NZ), c))
+    for k in range(1, LAYERS):
+        greeted += [(sec(k), t * 2 + c), (sec(k), t * 2 + 1 - c)]
+    greeted += [partner, prev_chip, next_chip]
+    for k, device in enumerate(greeted):
+
+        def greet():
+            pl.semaphore_signal(barrier, inc=1, device_id=device, device_id_type=MESH)
+
+        if k == 0:
+            pl.when(d != c)(greet)
+        else:
+            greet()
     for load in loads:
         load.start()
 
-    edge = pl.multiple_of(80 * c, 16)
-    for layer in range(LAYERS):
-        S[layer, :, pl.ds(edge, 16), :] = jnp.zeros((ROWS, 16, CH), BF16)
-        R[layer, :, 22:24] = jnp.zeros((GROUPS, 2, GROUP, CH), BF16)
-
-        @pl.when(t == 0)
-        def _():
-            R[layer, :, 0:RAD] = jnp.zeros((GROUPS, RAD, GROUP, CH), BF16)
-
-        @pl.when(t == NY * NZ - 1)
-        def _():
-            R[layer, :, 15:22] = jnp.zeros((GROUPS, RAD, GROUP, CH), BF16)
-
-    rc = row_coef[0].astype(F32)
-    for i in range(4):
-        RC[s, c * 4 + i] = jnp.concatenate([rc[:, i, :], jnp.zeros((1, 128), F32)], axis=0)
-    PB[s] = jnp.zeros((8, HID), F32)
-    PB[s, 0:1, :] = bias[...].astype(F32)
-    PB[s, 1:2, 0:CH] = gain[...].astype(F32)
-    CS[...] = jnp.zeros(CS.shape, F32)
-    CS[0:TAPS, :] = col_coef[0, 0].astype(F32)
+    CS[TAPS:, :] = jnp.zeros((128 - TAPS, 512), F32)
+    small[0].wait()
+    CS[0:TAPS, :] = ccv[...].astype(F32)
     for q in range(4):
         CT[128 * q : 128 * (q + 1), :] = CS[:, 128 * q : 128 * (q + 1)].T
     for zz in range(NZ):
@@ -109,8 +107,14 @@
         for r in range(1, ROWS):
             total = total + pltpu.roll(CT[pl.ds(8 * zz + r, 8, stride=64), :], 16 * r, 1)
         ZS[zz] = total
-
-    pl.semaphore_wait(barrier, len(greeted))
+    small[1].wait()
+    rc = rcv[...].astype(F32)
+    for i in range(4):
+        RC[s, c * 4 + i] = jnp.concatenate(
+            [rc[:, i, :], jnp.zeros((1, 128), F32)], axis=0
+        ).astype(BF16)
+
+    pl.semaphore_wait(barrier, len(greeted) - 1 + jnp.where(d != c, 1, 0))
 
     started = []
 
@@ -136,8 +140,6 @@
             partner,
         )
     )
-    for k in range(1, LAYERS):
-        go(remote(PB.at[s], PB.at[s], pbs.at[k], pbr.at[s], (sec(k), p)))
     wi_half, wo_half = pl.ds(c * 128, 128), pl.ds(c * 256, 256)
     wi_other, wo_other = pl.ds((1 - c) * 128, 128), pl.ds((1 - c) * 256, 256)
     up, down = (sec(1), p), (sec(3), p)
@@ -147,6 +149,32 @@
             dst = (WI.at[s, wi_half], WO.at[s, wo_half])[piece]
             go(remote(src, dst, ws.at[k, piece], wr.at[s, piece], device))
 
+    for load in small[2:4]:
+        load.wait()
+    PB[s] = jnp.zeros((8, HID), F32)
+    PB[s, 0:1, :] = bv[...].astype(F32)
+    PB[s, 1:2, 0:CH] = gv[...].astype(F32)
+    for k in range(1, LAYERS):
+        go(remote(PB.at[s], PB.at[s], pbs.at[k], pbr.at[s], (sec(k), p)))
+
+    edge = pl.multiple_of(80 * c, 16)
+
+    def clear(layer, carry):
+        S[layer, :, pl.ds(edge, 16), :] = jnp.zeros((ROWS, 16, CH), BF16)
+        R[layer, :, 22:24] = jnp.zeros((GROUPS, 2, GROUP, CH), BF16)
+
+        @pl.when(t == 0)
+        def _():
+            R[layer, :, 0:RAD] = jnp.zeros((GROUPS, RAD, GROUP, CH), BF16)
+
+        @pl.when(t == NY * NZ - 1)
+        def _():
+            R[layer, :, 15:22] = jnp.zeros((GROUPS, RAD, GROUP, CH), BF16)
+
+        return carry
+
+    lax.fori_loop(0, LAYERS, clear, 0)
+
     def got_rows(layer):
         for h in range(2):
 
@@ -158,7 +186,7 @@
     lane = lax.broadcasted_iota(jnp.int32, (HALF, 128), 1)
 
     def build_rows(layer):
-        TT[...] = RC[layer].reshape(128, 128).T
+        TT[...] = RC[layer].astype(F32).reshape(128, 128).T
         taps = TT[pl.ds(pl.multiple_of(HALF * c, HALF), HALF), :]
         for i in range(ROWS):
             kept = jnp.where(lane // 16 == i, taps, 0.0)
@@ -215,26 +243,20 @@
         def _():
             halo(layer, g, 1).wait_recv()
 
-    got_rows(0)
-    build_rows(0)
-    loads[0].wait()
-    their_rows = pl.ds((1 - c) * 4, 4)
-    remote(
-        raster.at[s, :, pl.ds(theirs, 80), :],
-        S.at[0, their_rows, pl.ds(mine_to, 80), :],
-        ras,
-        rar,
-        partner,
-    ).wait_recv()
-    for step in range(GROUPS):
-        send_row(0, order(step))
-
+    def weight_from(layer, piece):
+        ref = (WI.at[layer, wi_half], WO.at[layer, wo_half])[piece]
+        return remote(ref, ref, ws.at[0, 0], wr.at[layer, piece], partner)
+
+    def pass_on(layer, piece, k):
+        ref = (WI.at[layer, wi_half], WO.at[layer, wo_half])[piece]
+        go(remote(ref, ref, vs.at[k, piece], vr.at[layer, piece], partner))
+
+    below, above, across = sec(3), sec(1), sec(2)
     ZB[z] = ZS[z]
     for k in range(1, NZ):
         remote(
             ZS.at[0], ZB.at[lax.rem(z + NZ - k, NZ)], zs.at[0], zr.at[k], partner
         ).wait_recv()
-    d, gy = y // 4, y % 4
     for j in range(NY):
         yy = lax.rem(y + j, NY)
         YS[j] = ZB[pl.ds(0, NZ), yy, :]
@@ -262,15 +284,6 @@
 
                 own_y = copy
 
-    def weight_from(layer, piece):
-        ref = (WI.at[layer, wi_half], WO.at[layer, wo_half])[piece]
-        return remote(ref, ref, ws.at[0, 0], wr.at[layer, piece], partner)
-
-    def pass_on(layer, piece, k):
-        ref = (WI.at[layer, wi_half], WO.at[layer, wo_half])[piece]
-        go(remote(ref, ref, vs.at[k, piece], vr.at[layer, piece], partner))
-
-    below, above, across = sec(3), sec(1), sec(2)
     weight_from(below, 0).wait_recv()
     ref = WI.at[below, wi_half]
     go(remote(ref, ref, fs.at[0], wr.at[below, 0], up))
@@ -279,13 +292,33 @@
     go(remote(ref, ref, fs.at[1], wr.at[above, 1], down))
     pass_on(below, 0, 0)
     pass_on(above, 1, 1)
+    got_rows(0)
+    build_rows(0)
+    loads[0].wait()
+    their_rows = pl.ds((1 - c) * 4, 4)
+    remote(
+        raster.at[s, :, pl.ds(theirs, 80), :],
+        S.at[0, their_rows, pl.ds(mine_to, 80), :],
+        ras,
+        rar,
+        partner,
+    ).wait_recv()
+    def first_rows(step, carry):
+        send_row(0, order(step))
+        return carry
+
+    lax.fori_loop(0, GROUPS, first_rows, 0)
+
     weight_from(below, 1).wait_recv()
     pass_on(below, 1, 0)
     weight_from(above, 0).wait_recv()
     pass_on(above, 0, 1)
-    for l in range(1, LAYERS):
+    def later_rows(l, carry):
         got_rows(l)
         build_rows(l)
+        return carry
+
+    lax.fori_loop(1, LAYERS, later_rows, 0)
     for piece in range(2):
         weight_from(across, piece).wait_recv()
         pass_on(across, piece, 2)
@@ -366,26 +399,41 @@
 
     got_cols(0)
     build_cols(0)
-    for layer in range(LAYERS):
-        if layer > 0:
+    def layer_step(layer, carry):
+        @pl.when(layer > 0)
+        def _():
             ref = S.at[layer, :, pl.ds(edge_in, 16), :]
             remote(ref, ref, ss.at[layer], sr.at[layer], partner).wait_recv()
             send_row(layer, order(GROUPS - 1))
+
         got_weights(layer)
-        if layer + 1 < LAYERS:
+
+        @pl.when(layer + 1 < LAYERS)
+        def _():
             got_cols(layer + 1)
             build_cols(layer + 1)
-        for step in range(GROUPS):
+
+        def group_step(step, carry):
             g = order(step)
             got_halos(layer, g)
             dense(layer, g)
-            if layer + 1 < LAYERS:
-                if step == GROUPS - 1:
-                    go(edge_copy(layer + 1))
-                if step > 0:
-                    send_row(layer + 1, order(step - 1))
-
-    weights = jnp.broadcast_to(readout[...].astype(F32).reshape(1, CH), (8, CH))
+
+            @pl.when(jnp.logical_and(layer + 1 < LAYERS, step == GROUPS - 1))
+            def _():
+                edge_copy(layer + 1).start()
+
+            @pl.when(jnp.logical_and(layer + 1 < LAYERS, step > 0))
+            def _():
+                send_row(layer + 1, order(step - 1))
+
+            return carry
+
+        return lax.fori_loop(0, GROUPS, group_step, carry)
+
+    lax.fori_loop(0, LAYERS, layer_step, 0)
+
+    small[4].wait()
+    weights = jnp.broadcast_to(rv[...].astype(F32).reshape(1, CH), (8, CH))
     which = lax.broadcasted_iota(jnp.int32, (8, CH), 0)
     logits = jnp.zeros((8, HALF), F32)
     for i in range(ROWS):
@@ -410,7 +458,11 @@
     def _():
         own_y.wait_send()
 
-    for layer in range(LAYERS):
+    def drain(layer, carry):
+        @pl.when(layer > 0)
+        def _():
+            edge_copy(layer).wait_send()
+
         for g in range(GROUPS):
 
             @pl.when(not_first)
@@ -420,6 +472,10 @@
             @pl.when(not_last)
             def _():
                 halo(layer, g, 1).wait_send()
+
+        return carry
+
+    lax.fori_loop(0, LAYERS, drain, 0)
 
 
 def on_device(raster, row_coef, col_coef, norm_gain, weight_in, bias_in, weight_out, readout):
@@ -429,16 +485,21 @@
     return pl.pallas_call(
         kernel,
         out_shape=jax.ShapeDtypeStruct((1, 4, 128), F32),
-        in_specs=[anywhere, vmem, vmem, vmem, anywhere, vmem, anywhere, vmem],
+        in_specs=[anywhere] * 8,
         out_specs=vmem,
         scratch_shapes=[
+            pltpu.VMEM((TAPS, 4, 128), BF16),
+            pltpu.VMEM((TAPS, 512), BF16),
+            pltpu.VMEM((1, CH), BF16),
+            pltpu.VMEM((1, HID), BF16),
+            pltpu.VMEM((CH,), BF16),
             pltpu.VMEM((LAYERS + 1, ROWS, 96, CH), BF16),
             pltpu.VMEM((LAYERS, GROUPS, 24, GROUP, CH), BF16),
             pltpu.VMEM((LAYERS, GROUPS, ROWS, GROUP, 128), BF16),
             pltpu.VMEM((LAYERS, GROUPS, 128, BAND), BF16),
             pltpu.VMEM((LAYERS, CH, HID), BF16),
             pltpu.VMEM((LAYERS, HID, CH), BF16),
-            pltpu.VMEM((LAYERS, ROWS, 16, 128), F32),
+            pltpu.VMEM((LAYERS, ROWS, 16, 128), BF16),
             pltpu.VMEM((128, 128), F32),
             pltpu.VMEM((128, 512), F32),
             pltpu.VMEM((512, 128), F32),
@@ -450,7 +511,7 @@
             pltpu.VMEM((LAYERS, 8, HID), F32),
             pltpu.VMEM((2, 8, 128), F32),
             pltpu.VMEM((8, 128), F32),
-            dma((3,)),
+            dma((8,)),
             dma((NZ,)), dma((NZ,)),
             dma((LAYERS, NY)), dma((LAYERS, GROUPS, 2)),
             dma((7,)), dma((LAYERS, 2)),

time: 60.9 us -> 58.7 us (0.964)
  the two profiles are of different devices: /device:TPU:15 before, /device:TPU:8 now
where the time goes in v3:
time: 58.7 us; the launch traced here: 57.9 us
  Pallas kernels  56.6 us (96%)
  local copies, waits for them, and re-layouts  1.26 us (2%)
    pallas_call x1, Pallas kernels, on_device(): pl.pallas_call(kernel, out_shape=jax.ShapeDtypeStruct((1, 4, 128), F32),...  56.6 us
    unnamed x1, local copies, waits for them, and re-layouts  1.26 us

profile of v3, /device:TPU:8, one launch (start us, length us, event | category | flops | bytes accessed | tf_op | source)
XLA Modules:
  0.0 57.9 jit_solution(2339089224857220143)
XLA Ops:
  0.0 56.6 %forecast.1 = f32[1,4,128]{2,1,0:T(4,128)} custom-call(bf16[4,4,128,256]{3,2,1,0:T(8,128)(2,1)} %raster.1, bf16[1,15,4,128]{3,2,1,0:T(4,128)(2,1)} %row_coef.1, bf16[1,1,15,512]{3,2,1,0:T(8,128)(2,1)} %bitcast.1, bf16[1,256]{1,0:T(2,128)(2,1)} %gain.1, bf16[1,256,512]{2,1,0:T(8,128)(2,1)} %w_in.1, bf16[1,512]{1,0:T(2,128)(2,1)} %bias.1, ...), custom_call_target="tpu_custom_call" | custom-call | tf_op jit(solution)/shard_map/forecast/pallas_call | solution.py:485
  56.6 1.3 %copy.10 = f32[1,4,128]{2,1,0:T(4,128)} copy(f32[1,4,128]{2,1,0:T(4,128)} %forecast.1) | data formatting | bytes 4096

commit v4 on v3

--- a/solution.py
+++ b/solution.py
@@ -260,8 +260,8 @@
     for j in range(NY):
         yy = lax.rem(y + j, NY)
         YS[j] = ZB[pl.ds(0, NZ), yy, :]
-    for k in range(LAYERS):
-        for j in range(NY):
+    for k in (2, 1, 3, 0):
+        for j in (4, 3, 5, 2, 6, 1, 7, 0):
             yy = lax.rem(y + j, NY)
             copy = remote(
                 YS.at[j],
@@ -446,36 +446,39 @@
     values = jax.nn.softplus(jnp.concatenate([logits, logits], axis=1))
     DS[0] = values
     DS[1] = pltpu.roll(values, 4, 0)
-    go(remote(DS.at[1 - c], DR, ds, dr, partner))
+    to_partner = remote(DS.at[1 - c], DR, ds, dr, partner)
+    to_partner.start()
+
+    for copy in started:
+        copy.wait_send()
+
+    @pl.when(d != c)
+    def _():
+        own_y.wait_send()
+
+    def drain(layer, carry):
+        @pl.when(layer > 0)
+        def _():
+            edge_copy(layer).wait_send()
+
+        for g in range(GROUPS):
+
+            @pl.when(not_first)
+            def _():
+                halo(layer, g, 0).wait_send()
+
+            @pl.when(not_last)
+            def _():
+                halo(layer, g, 1).wait_send()
+
+        return carry
+
+    lax.fori_loop(0, LAYERS, drain, 0)
+
     remote(DS.at[c], DR, ds, dr, partner).wait_recv()
     cols = lax.broadcasted_iota(jnp.int32, (8, 128), 1)
     out[0] = jnp.where(cols // HALF == c, DS[c], DR[...])[0:4]
-
-    for copy in started:
-        copy.wait_send()
-
-    @pl.when(d != c)
-    def _():
-        own_y.wait_send()
-
-    def drain(layer, carry):
-        @pl.when(layer > 0)
-        def _():
-            edge_copy(layer).wait_send()
-
-        for g in range(GROUPS):
-
-            @pl.when(not_first)
-            def _():
-                halo(layer, g, 0).wait_send()
-
-            @pl.when(not_last)
-            def _():
-                halo(layer, g, 1).wait_send()
-
-        return carry
-
-    lax.fori_loop(0, LAYERS, drain, 0)
+    to_partner.wait_send()
 
 
 def on_device(raster, row_coef, col_coef, norm_gain, weight_in, bias_in, weight_out, readout):

time: 58.7 us -> 58.5 us (level)
  no operation moved by 1% of the time
where the time goes in v4:
time: 58.5 us; the launch traced here: 57.8 us
  Pallas kernels  56.5 us (97%)
  local copies, waits for them, and re-layouts  1.26 us (2%)
    pallas_call x1, Pallas kernels, on_device(): pl.pallas_call(kernel, out_shape=jax.ShapeDtypeStruct((1, 4, 128), F32),...  56.5 us
    unnamed x1, local copies, waits for them, and re-layouts  1.26 us

profile of v4, /device:TPU:8, one launch (start us, length us, event | category | flops | bytes accessed | tf_op | source)
XLA Modules:
  0.0 57.8 jit_solution(12900614568750960305)
XLA Ops:
  0.0 56.5 %forecast.1 = f32[1,4,128]{2,1,0:T(4,128)} custom-call(bf16[4,4,128,256]{3,2,1,0:T(8,128)(2,1)} %raster.1, bf16[1,15,4,128]{3,2,1,0:T(4,128)(2,1)} %row_coef.1, bf16[1,1,15,512]{3,2,1,0:T(8,128)(2,1)} %bitcast.1, bf16[1,256]{1,0:T(2,128)(2,1)} %gain.1, bf16[1,256,512]{2,1,0:T(8,128)(2,1)} %w_in.1, bf16[1,512]{1,0:T(2,128)(2,1)} %bias.1, ...), custom_call_target="tpu_custom_call" | custom-call | tf_op jit(solution)/shard_map/forecast/pallas_call | solution.py:488
  56.5 1.3 %copy.10 = f32[1,4,128]{2,1,0:T(4,128)} copy(f32[1,4,128]{2,1,0:T(4,128)} %forecast.1) | data formatting | bytes 4096
